TPU v7x, 32 devices: a whole 2x2x4 slice. The times are simulated.
32 devices in a mesh: lat: 4 (over y, x), ord: 8 (over z, core).
Axes of the slice: x: 2, y: 2, z: 4, core: 2. Of those that a mesh axis runs over, the one named last changes fastest.
Arguments:
- heights: bfloat16 [512, 43200], P(('lat', 'ord')), may hold values from -1.5 to 1.5
- panels: bfloat16 [512, 5120, 128], P('lat', 'ord'), may hold values from -0.25 to 0.25
- ord_slot: int32 [5120], replicated, may hold values from 0 to 5119, each once
- cutoffs: int32 [5120], P('ord'), may hold values from 13360 to 21599
Outputs:
- gravity: float32 [512, 43200], P(('lat', 'ord'))
Inputs may be any that keep to these rules, and one draw needn't show every extreme that they name: `ord_slot`: a permutation of the order slots.
All inputs are finite; a program needn't handle non-finite values.
Results may differ from a plain program's by a relative error of at most 0.0039.
Values may be sent and summed in bfloat16 or wider, within the bound.
No kernel may reach another device: no remote copies, remote signals or barrier semaphores. Data moves between devices by JAX's collectives and lax.ppermute only.
A program may use at most 192 MiB of HBM per device.

v0:
```python
import math
import jax
import jax.numpy as jnp
from jax import lax
from jax.sharding import PartitionSpec as P

LON_SLOW = 180
LON_FAST = 240
ORDERS = 5120
DEG = 128
NMAX = 21600


def slow_tables(slow):
    index = jnp.arange(slow, dtype=jnp.int32)
    phase = index[:, None] * index[None, :] % slow
    angle = 2.0 * math.pi / slow * phase.astype(jnp.float32)
    return (jnp.cos(angle), jnp.sin(angle))


def twiddle_tables(slow, fast, blocks):
    total = slow * fast
    first = jnp.arange(slow, dtype=jnp.int32)[:, None, None]
    middle = jnp.arange(fast, dtype=jnp.int32)[None, :, None]
    last = jnp.arange(blocks, dtype=jnp.int32)[None, None, :]
    phase = (middle * first + slow * middle * last) % total
    angle = 2.0 * math.pi / total * phase.astype(jnp.float32)
    return (jnp.cos(angle), jnp.sin(angle))


def forward_spectra(values, slow, fast, orders):
    count = values.shape[0]
    grid = values.reshape(count, slow, fast)
    cosine, sine = slow_tables(slow)
    first_real = jnp.einsum("raj,ak->rkj", grid, cosine, precision=lax.Precision.HIGHEST)
    first_imag = -jnp.einsum("raj,ak->rkj", grid, sine, precision=lax.Precision.HIGHEST)
    blocks = orders // slow + 1
    twist_cos, twist_sin = twiddle_tables(slow, fast, blocks)
    joined = jnp.concatenate([first_real, first_imag], 2)
    table = jnp.concatenate(
        [jnp.concatenate([twist_cos, -twist_sin], 2), jnp.concatenate([twist_sin, twist_cos], 2)], 1
    )
    second = jnp.einsum("rkj,kjq->rkq", joined, table, precision=lax.Precision.HIGHEST)
    scale_in = 1.0 / math.sqrt(slow * fast)
    spec_real = (
        second[:, :, :blocks].transpose(0, 2, 1).reshape(count, blocks * slow)[:, 1 : orders + 1]
    )
    spec_imag = (
        second[:, :, blocks:].transpose(0, 2, 1).reshape(count, blocks * slow)[:, 1 : orders + 1]
    )
    return (spec_real * scale_in, spec_imag * scale_in)


def inverse_field(full_real, full_imag, slow, fast):
    count = full_real.shape[0]
    blocks = full_real.shape[1] // slow
    grid_real = full_real.reshape(count, blocks, slow).transpose(0, 2, 1)
    grid_imag = full_imag.reshape(count, blocks, slow).transpose(0, 2, 1)
    joined = jnp.concatenate([grid_real, grid_imag], 2)
    twist_cos, twist_sin = twiddle_tables(slow, fast, blocks)
    cos_turned = twist_cos.transpose(0, 2, 1)
    sin_turned = twist_sin.transpose(0, 2, 1)
    table = jnp.concatenate(
        [
            jnp.concatenate([cos_turned, sin_turned], 2),
            jnp.concatenate([-sin_turned, cos_turned], 2),
        ],
        1,
    )
    second = jnp.einsum("rkq,kqj->rkj", joined, table, precision=lax.Precision.HIGHEST)
    cosine, sine = slow_tables(slow)
    field = jnp.einsum("rkj,ka->raj", second[:, :, :fast], cosine, precision=lax.Precision.HIGHEST)
    field = field - jnp.einsum(
        "rkj,ka->raj", second[:, :, fast:], sine, precision=lax.Precision.HIGHEST
    )
    return field.reshape(count, slow * fast)


def fold_powers(terms, factors):
    slots = terms.shape[1]
    width = terms.shape[2]
    return jnp.sum(terms.reshape(3, 2, slots, width) * factors[:, None, None, :], axis=0)


def local(heights, panels, ord_slot, cutoffs):
    lat_count = lax.axis_size("lat")
    ord_count = lax.axis_size("ord")
    level = heights.astype(jnp.float32)
    cycle_dev = level.shape[0]
    square = level * level
    powers = jnp.concatenate([level, square, square * level], 0)
    spec_real, spec_imag = forward_spectra(powers, LON_SLOW, LON_FAST, ORDERS)
    picked = jnp.stack(
        [
            spec_real[:, ord_slot].reshape(3, cycle_dev, ORDERS),
            spec_imag[:, ord_slot].reshape(3, cycle_dev, ORDERS),
        ],
        1,
    )
    picked = picked.reshape(6, cycle_dev, ORDERS).astype(jnp.bfloat16)
    sums = jnp.einsum(
        "xrk,rkn->xkn",
        lax.all_to_all(picked, "ord", split_axis=2, concat_axis=1, tiled=True),
        panels,
        preferred_element_type=jnp.float32,
    )
    stride = (NMAX - ORDERS) // DEG
    degree_int = ORDERS + jnp.arange(DEG, dtype=jnp.int32) * stride
    degree = degree_int.astype(jnp.float32)
    factors = jnp.stack(
        [
            jnp.ones_like(degree),
            (degree + 2.0) / (2.0 * NMAX),
            (degree + 2.0) * (degree + 1.0) / (6.0 * NMAX * NMAX),
        ]
    )
    keep = (degree_int[None, :] <= cutoffs[:, None]).astype(jnp.float32)
    terms = fold_powers(sums, factors)
    total = lax.psum(terms, "lat")
    coeffs = (total * keep[None]).astype(jnp.bfloat16)
    synthesis = jnp.einsum("rkn,ckn->crk", panels, coeffs, preferred_element_type=jnp.float32)
    returned = lax.all_to_all(synthesis, "ord", split_axis=1, concat_axis=2, tiled=True)
    blocks = ORDERS // LON_SLOW + 1
    target = ord_slot + 1
    full_real = (
        jnp.zeros((cycle_dev, blocks * LON_SLOW), jnp.float32).at[:, target].set(returned[0])
    )
    full_imag = (
        jnp.zeros((cycle_dev, blocks * LON_SLOW), jnp.float32).at[:, target].set(returned[1])
    )
    field = inverse_field(full_real, full_imag, LON_SLOW, LON_FAST)
    cycles_all = cycle_dev * lat_count * ord_count
    return field * math.sqrt(cycles_all / (DEG * ORDERS))


def solution(mesh):
    return jax.shard_map(
        local,
        mesh=mesh,
        in_specs=(P(("lat", "ord"), None), P("lat", "ord", None), P(), P("ord")),
        out_specs=P(("lat", "ord"), None),
        check_vma=False,
    )
```

profile of v0, /device:TPU:1, one launch (start us, length us, event | category | flops | bytes accessed | tf_op | source)
XLA Modules:
  0.0 486.3 jit_solution(7475713609874748307)
XLA Ops:
  8.5 3.5 pad_maximum_fusion.1
  12.1 11.4 %reshape.129 = f32[48,180,240]{2,1,0:T(8,128)} reshape(f32[48,43200]{1,0:T(8,128)} %pad_maximum_fusion.1) | data formatting | bytes 16588800 | tf_op jit(solution)/shard_map/reshape | solution.py:33
  23.5 13.0 %convolution_bitcast_fusion = f32[48,180,240]{2,1,0:T(8,128)S(1)} fusion(f32[48,180,240]{2,1,0:T(8,128)} %reshape.129), kind=kOutput, calls=%fused_computation.48 | convolution fusion | flops 4479267840 | bytes 16588800 | tf_op jit(solution)/shard_map/raj,ak->rkj/dot_general | solution.py:35
  36.5 10.0 %negate_bitcast_fusion = f32[48,180,240]{2,1,0:T(8,128)S(1)} fusion(f32[48,180,240]{2,1,0:T(8,128)S(1)} %copy-done), kind=kOutput, calls=%fused_computation.26 | convolution fusion | flops 4481341440 | bytes 16588800 | tf_op jit(solution)/shard_map/raj,ak->rkj/dot_general | solution.py:36
  46.5 7.9 %pad_maximum_fusion = f32[48,180,480]{2,1,0:T(8,128)} fusion(f32[48,180,240]{2,1,0:T(8,128)S(1)} %negate_bitcast_fusion, f32[48,180,240]{2,1,0:T(8,128)S(1)} %convolution_bitcast_fusion), kind=kLoop, calls=%fused_computation.24 | loop fusion | flops 4147200 | bytes 33177600 | tf_op jit(solution)/shard_map/concatenate | solution.py:39
  54.4 26.4 %fusion.50 = (f32[180,240,29]{1,2,0:T(8,128)}, f32[180,240,29]{1,2,0:T(8,128)}, f32[180,240,29]{1,2,0:T(8,128)}) fusion(s32[240,29]{0,1:T(8,128)S(1)} %iota_multiply_fusion.1, s32[180,240]{1,0:T(8,128)S(1)} %iota_multiply_fusion), kind=kLoop, calls=%fused_computation.60 | loop fusion | flops 12528000 | bytes 15234240 | tf_op jit(solution)/shard_map/neg | solution.py:41
  80.8 38.7 %fusion.42 = f32[48,180,58]{2,0,1:T(8,128)S(1)} fusion(f32[48,180,480]{2,1,0:T(8,128)} %pad_maximum_fusion, f32[180,240,29]{1,2,0:T(8,128)} %get-tuple-element.15, f32[180,240,29]{1,2,0:T(8,128)} %get-tuple-element.14, f32[180,240,29]{1,2,0:T(8,128)} %get-tuple-element.13), kind=kOutput, calls=%fused_computation.57 | convolution fusion | flops 2901484800 | bytes 33626880 | tf_op jit(solution)/shard_map/rkj,kjq->rkq/dot_general | solution.py:43
  119.6 4.8 slice_bitcast_fusion.1
  124.4 4.4 copy.110
  130.5 2.1 slice_multiply_fusion.1
  132.6 15.1 %gather_fusion = bf16[5120,48]{1,0:T(8,128)(2,1)S(1)} fusion(bf16[48,5120]{0,1:T(8,128)(2,1)S(1)} %slice_multiply_fusion.1, s32[5120]{0:T(1024)S(1)} %get-tuple-element.19), kind=kCustom, calls=%fused_computation | custom fusion | bytes 1003520 | tf_op jit(solution)/shard_map/gather | solution.py:95
  148.3 4.4 copy.111
  156.5 15.1 %gather_fusion.1 = bf16[5120,48]{1,0:T(8,128)(2,1)S(1)} fusion(bf16[48,5120]{0,1:T(8,128)(2,1)S(1)} %slice_multiply_fusion, s32[5120]{0:T(1024)S(1)} %get-tuple-element.19), kind=kCustom, calls=%fused_computation.1 | custom fusion | bytes 1003520 | tf_op jit(solution)/shard_map/gather | solution.py:96
  172.4 8.2 %copy.90 = bf16[6,16,5120]{1,0,2:T(8,128)(2,1)} copy(bf16[6,16,5120]{2,1,0:T(8,128)(2,1)S(1)} %bitcast.72) | data formatting | bytes 1966080 | tf_op jit(solution)/shard_map/convert_element_type | solution.py:100
  180.6 11.5 %reshape.179 = bf16[8,2,30720]{2,1,0:T(2,128)(2,1)} reshape(bf16[5120,6,16]{2,1,0:T(8,128)(2,1)} %bitcast.69) | data formatting | bytes 1966080
  192.0 6.4 %all-to-all-start = ((bf16[8,2,30720]{2,1,0:T(2,128)(2,1)}), bf16[8,2,30720]{2,1,0:T(2,128)(2,1)S(1)}, u32[]{:S(2)}, u32[]{:S(2)}) async-start(bf16[8,2,30720]{2,1,0:T(2,128)(2,1)} %reshape.179), calls=%async_computation | async-start | bytes 1966080 | tf_op jit(solution)/shard_map/all_to_all | solution.py:103
  198.4 24.2 %all-to-all-done = bf16[8,2,30720]{2,1,0:T(2,128)(2,1)S(1)} async-done(((bf16[8,2,30720]{2,1,0:T(2,128)(2,1)}), bf16[8,2,30720]{2,1,0:T(2,128)(2,1)S(1)}, u32[]{:S(2)}, u32[]{:S(2)}) %all-to-all-start) | async-done | bytes 983072 | tf_op jit(solution)/shard_map/all_to_all | solution.py:103
  222.6 11.0 %reshape.180 = bf16[5120,6,16]{2,1,0:T(8,128)(2,1)} reshape(bf16[8,2,30720]{2,1,0:T(2,128)(2,1)S(1)} %all-to-all-done) | data formatting | bytes 1966080
  233.6 8.5 %copy.92 = bf16[6,8,16,640]{3,2,1,0:T(8,128)(2,1)S(1)} copy(bf16[6,8,16,640]{2,0,3,1:T(8,128)(2,1)} %bitcast.70) | data formatting | bytes 1966080 | tf_op jit(solution)/shard_map/all_to_all | solution.py:103
  243.4 26.1 %fusion.51 = f32[6,640,128]{2,0,1:T(8,128)S(1)} fusion(bf16[6,128,640]{1,0,2:T(8,128)(2,1)S(1)} %copy.93, bf16[128,640,128]{2,1,0:T(8,128)(2,1)} %param.5), kind=kOutput, calls=%fused_computation.61 | convolution fusion | flops 125829120 | bytes 23920640 | tf_op jit(solution)/shard_map/xrk,rkn->xkn/dot_general | solution.py:101
  271.0 45.9 %all-reduce.2.cloned.1.call-done = f32[2,640,128]{2,1,0:T(8,128)} async-done(((f32[2,640,128]{2,1,0:T(8,128)}), f32[2,640,128]{2,1,0:T(8,128)}) %all-reduce.2.cloned.1.call-update) | async-done | bytes 655376 | tf_op jit(solution)/shard_map/psum | solution.py:119
  318.1 50.4 %fusion.61 = f32[2,128,640]{1,0,2:T(2,128)S(1)} fusion(bf16[128,640,128]{2,1,0:T(8,128)(2,1)} %param.5, bf16[2,640,128]{2,1,0:T(8,128)(2,1)S(1)} %multiply_convert_fusion), kind=kOutput, calls=%fused_computation.73 | convolution fusion | flops 41943040 | bytes 21954560 | tf_op jit(solution)/shard_map/rkn,ckn->crk/dot_general | solution.py:121
  369.9 5.3 %all-to-all-start.1 = ((f32[2,128,640]{2,0,1:T(2,128)}), f32[2,128,640]{2,0,1:T(2,128)S(1)}, u32[]{:S(2)}, u32[]{:S(2)}) async-start(f32[2,128,640]{2,0,1:T(2,128)} %copy.98), calls=%async_computation.1 | async-start | bytes 1310720 | tf_op jit(solution)/shard_map/all_to_all | solution.py:122
  375.2 26.6 %fusion.31 = (f32[180,29,240]{2,1,0:T(8,128)}, f32[180,29,240]{2,1,0:T(8,128)}, f32[180,29,240]{2,1,0:T(8,128)}) fusion(s32[29,240]{1,0:T(8,128)S(1)} %iota_multiply_fusion.2, s32[180,240]{1,0:T(8,128)S(1)} %iota_multiply_fusion), kind=kLoop, calls=%fused_computation.42 | loop fusion | flops 12528000 | bytes 15234240 | tf_op jit(solution)/shard_map/sin | solution.py:28
  401.9 2.2 copy.101
  404.2 14.0 %scatter_custom_fusion = f32[16,5220]{0,1:T(8,128)S(1)} fusion(s32[5120]{0:T(1024)S(1)} %get-tuple-element.20, f32[5120,16]{1,0:T(8,128)} %copy.101, f32[]{:T(128)} %constant.52.clone.1), kind=kCustom, calls=%fused_computation.69 | custom fusion | bytes 334592 | tf_op jit(solution)/shard_map/scatter | solution.py:126
  421.7 2.2 copy.105
  423.9 14.0 %scatter_custom_fusion.1 = f32[16,5220]{0,1:T(8,128)S(1)} fusion(s32[5120]{0:T(1024)S(1)} %get-tuple-element.20, f32[5120,16]{1,0:T(8,128)} %copy.105, f32[]{:T(128)} %constant.52.clone.1), kind=kCustom, calls=%fused_computation.67 | custom fusion | bytes 334592 | tf_op jit(solution)/shard_map/scatter | solution.py:129
  441.4 24.1 %fusion.39 = f32[16,180,480]{2,0,1:T(8,128)S(1)} fusion(f32[180,29,240]{2,1,0:T(8,128)} %get-tuple-element.18, f32[180,29,240]{2,1,0:T(8,128)} %get-tuple-element.17, f32[180,29,240]{2,1,0:T(8,128)} %get-tuple-element.16, f32[16,180,29]{2,0,1:T(8,128)} %bitcast.80, f32[16,180,29]{2,0,1:T(8,128)} %bitcast.79), kind=kOutput, calls=%fused_computation.56 | convolution fusion | flops 977351040 | bytes 21231360 | tf_op jit(solution)/shard_map/rkq,kqj->rkj/dot_general | solution.py:70
  466.6 4.9 %fusion.35 = f32[180,16,240]{2,0,1:T(8,128)S(1)} fusion(f32[16,180,240]{2,0,1:T(8,128)S(1)} %get-tuple-element.6), kind=kOutput, calls=%fused_computation.49 | convolution fusion | flops 1493283584 | bytes 5529600 | tf_op jit(solution)/shard_map/rkj,ka->raj/dot_general | solution.py:73
  471.5 5.1 %multiply_bitcast_fusion = f32[16,180,240]{2,1,0:T(8,128)S(1)} fusion(f32[180,16,240]{2,0,1:T(8,128)S(1)} %fusion.35, f32[16,180,240]{2,0,1:T(8,128)S(1)} %get-tuple-element.5), kind=kOutput, calls=%fused_computation.53 | convolution fusion | flops 1494665984 | bytes 8294400 | tf_op jit(solution)/shard_map/rkj,ka->raj/dot_general | solution.py:72
  476.6 2.5 mul.334
  (46 shorter events, 22.3 us)
Async XLA Ops:
  6.5 1.8 copy-start.1
  23.5 13.0 %copy-start = (f32[48,180,240]{2,1,0:T(8,128)S(1)}, f32[48,180,240]{2,1,0:T(8,128)}, u32[]{:S(2)}) copy-start(f32[48,180,240]{2,1,0:T(8,128)} %reshape.129) | copy-start | bytes 24883204
  128.8 3.8 copy-start.2
  192.0 30.6 %all-to-all-start = ((bf16[8,2,30720]{2,1,0:T(2,128)(2,1)}), bf16[8,2,30720]{2,1,0:T(2,128)(2,1)S(1)}, u32[]{:S(2)}, u32[]{:S(2)}) async-start(bf16[8,2,30720]{2,1,0:T(2,128)(2,1)} %reshape.179), calls=%async_computation | async-start | bytes 1966080 | tf_op jit(solution)/shard_map/all_to_all | solution.py:103
  198.4 118.6 %all-reduce.2.cloned.1.call-start = ((), (), s32[]{:S(2)}) async-start(), calls=%async_computation.2 | async-start | bytes 1310720 | tf_op jit(solution)/shard_map/psum | solution.py:119
  269.4 1.4 copy-start.3
  369.9 32.0 %all-to-all-start.1 = ((f32[2,128,640]{2,0,1:T(2,128)}), f32[2,128,640]{2,0,1:T(2,128)S(1)}, u32[]{:S(2)}, u32[]{:S(2)}) async-start(f32[2,128,640]{2,0,1:T(2,128)} %copy.98), calls=%async_computation.1 | async-start | bytes 1310720 | tf_op jit(solution)/shard_map/all_to_all | solution.py:122
Sparse Core Ops, SparseCore 0:
  271.0 45.9 all-reduce.1
where the time goes:
time: 493 us; the launch traced here: 486 us
  matrix products  172 us (35%)
  local copies, waits for them, and re-layouts  145 us (29%)
  other arithmetic  73.1 us (15%)
  waiting for transfers between devices  70.1 us (14%)
  between operations  14 us (3%)
  starting transfers between devices  11.7 us (2%)
    dot_general x1, matrix products, local(): jnp.einsum('rkn,ckn->crk', panels, coeffs, preferred_element_type=jnp.flo...  50.4 us
    psum x1, waiting for transfers between devices, local(): total = lax.psum(terms, 'lat')  45.9 us
    dot_general x1, matrix products, forward_spectra(): jnp.einsum('rkj,kjq->rkq', joined, table, precision=lax.Precision.HIGHEST)  38.7 us
    scatter x4, local copies, waits for them, and re-layouts, local(): jnp.zeros((cycle_dev, blocks * LON_SLOW), jnp.float32).at[:, target]  29.5 us
    sin x1, other arithmetic, twiddle_tables(): return (jnp.cos(angle), jnp.sin(angle))  26.6 us
    neg x1, other arithmetic, forward_spectra(): -twist_sin  26.4 us
    dot_general x1, matrix products, local(): jnp.einsum('xrk,rkn->xkn', lax.all_to_all(picked, 'ord', split_axis=2, co...  26.1 us
    all_to_all x1, waiting for transfers between devices, local(): lax.all_to_all(picked, 'ord', split_axis=2, concat_axis=1, tiled=True)  24.2 us
  transfers between devices with their start and end apart: 3, of which 2 were waited for; matrix products, arithmetic and copies ran while one was open for 6% of the time, Pallas kernels for 0%

commit v1 on v0

--- a/solution.py
+++ b/solution.py
@@ -100,7 +100,10 @@
     picked = picked.reshape(6, cycle_dev, ORDERS).astype(jnp.bfloat16)
     sums = jnp.einsum(
         "xrk,rkn->xkn",
-        lax.all_to_all(picked, "ord", split_axis=2, concat_axis=1, tiled=True),
+        jnp.concatenate(
+            lax.all_to_all(jnp.stack(jnp.split(picked, lax.axis_size("ord"), axis=2)), "ord", 0, 0),
+            axis=1,
+        ),
         panels,
         preferred_element_type=jnp.float32,
     )

time: 493 us -> 459 us (0.931)
  local copies, waits for them, and re-layouts: 145 us -> 112 us
    unnamed x12 -> x17, local copies, waits for them, and re-layouts: 22.5 us -> 4.69 us
    all_to_all x2 -> x0, local copies, waits for them, and re-layouts: 9.82 us -> none  [local(): lax.all_to_all(picked, 'ord', split_axis=2, concat_axis=1, tiled=True)]
    convert_element_type x1 -> x0, local copies, waits for them, and re-layouts: 8.16 us -> none  [local(): picked = picked.reshape(6, cycle_dev, ORDERS).astype(jnp.bfloat16)]
where the time goes in v1:
time: 459 us; the launch traced here: 453 us
  matrix products  172 us (37%)
  local copies, waits for them, and re-layouts  112 us (24%)
  other arithmetic  73.1 us (16%)
  waiting for transfers between devices  70.1 us (15%)
  between operations  14 us (3%)
  starting transfers between devices  11.7 us (3%)
    dot_general x1, matrix products, local(): jnp.einsum('rkn,ckn->crk', panels, coeffs, preferred_element_type=jnp.flo...  50.4 us
    psum x1, waiting for transfers between devices, local(): total = lax.psum(terms, 'lat')  45.9 us
    dot_general x1, matrix products, forward_spectra(): jnp.einsum('rkj,kjq->rkq', joined, table, precision=lax.Precision.HIGHEST)  38.5 us
    scatter x4, local copies, waits for them, and re-layouts, local(): jnp.zeros((cycle_dev, blocks * LON_SLOW), jnp.float32).at[:, target]  29.5 us
    sin x1, other arithmetic, twiddle_tables(): return (jnp.cos(angle), jnp.sin(angle))  26.6 us
    neg x1, other arithmetic, forward_spectra(): -twist_sin  26.4 us
    dot_general x1, matrix products, local(): jnp.einsum('xrk,rkn->xkn', jnp.concatenate(lax.all_to_all(jnp.stack(jnp.s...  26.1 us
    all_to_all x1, waiting for transfers between devices, local(): lax.all_to_all(jnp.stack(jnp.split(picked, lax.axis_size('ord'), axis=2))...  24.2 us
  transfers between devices with their start and end apart: 3, of which 2 were waited for; matrix products, arithmetic and copies ran while one was open for 6% of the time, Pallas kernels for 0%

profile of v1, /device:TPU:1, one launch (start us, length us, event | category | flops | bytes accessed | tf_op | source)
XLA Modules:
  0.0 452.8 jit_solution(8767919722951703207)
XLA Ops:
  6.5 1.8 convert_multiply_fusion.1
  8.5 3.5 pad_maximum_fusion.1
  12.1 11.4 %reshape.135 = f32[48,180,240]{2,1,0:T(8,128)} reshape(f32[48,43200]{1,0:T(8,128)} %pad_maximum_fusion.1) | data formatting | bytes 16588800 | tf_op jit(solution)/shard_map/reshape | solution.py:33
  23.5 13.0 %convolution_bitcast_fusion = f32[48,180,240]{2,1,0:T(8,128)S(1)} fusion(f32[48,180,240]{2,1,0:T(8,128)} %reshape.135), kind=kOutput, calls=%fused_computation.48 | convolution fusion | flops 4479267840 | bytes 16588800 | tf_op jit(solution)/shard_map/raj,ak->rkj/dot_general | solution.py:35
  36.5 10.0 %negate_bitcast_fusion = f32[48,180,240]{2,1,0:T(8,128)S(1)} fusion(f32[48,180,240]{2,1,0:T(8,128)S(1)} %copy-done), kind=kOutput, calls=%fused_computation.26 | convolution fusion | flops 4481341440 | bytes 16588800 | tf_op jit(solution)/shard_map/raj,ak->rkj/dot_general | solution.py:36
  46.5 7.9 %pad_maximum_fusion = f32[48,180,480]{2,1,0:T(8,128)} fusion(f32[48,180,240]{2,1,0:T(8,128)S(1)} %negate_bitcast_fusion, f32[48,180,240]{2,1,0:T(8,128)S(1)} %convolution_bitcast_fusion), kind=kLoop, calls=%fused_computation.24 | loop fusion | flops 4147200 | bytes 33177600 | tf_op jit(solution)/shard_map/concatenate | solution.py:39
  54.4 26.4 %fusion.50 = (f32[180,240,29]{1,2,0:T(8,128)}, f32[180,240,29]{1,2,0:T(8,128)}, f32[180,240,29]{1,2,0:T(8,128)}) fusion(s32[240,29]{0,1:T(8,128)S(1)} %iota_multiply_fusion.1, s32[180,240]{1,0:T(8,128)S(1)} %iota_multiply_fusion), kind=kLoop, calls=%fused_computation.60 | loop fusion | flops 12528000 | bytes 15234240 | tf_op jit(solution)/shard_map/neg | solution.py:41
  80.8 38.5 %fusion.42 = f32[48,180,58]{2,0,1:T(8,128)S(1)} fusion(f32[48,180,480]{2,1,0:T(8,128)} %pad_maximum_fusion, f32[180,240,29]{1,2,0:T(8,128)} %get-tuple-element.15, f32[180,240,29]{1,2,0:T(8,128)} %get-tuple-element.14, f32[180,240,29]{1,2,0:T(8,128)} %get-tuple-element.13), kind=kOutput, calls=%fused_computation.57 | convolution fusion | flops 2901484800 | bytes 33626880 | tf_op jit(solution)/shard_map/rkj,kjq->rkq/dot_general | solution.py:43
  119.4 4.8 %slice_bitcast_fusion.1 = (f32[48,29,180]{1,0,2:T(8,128)}, f32[48,29,180]{1,0,2:T(8,128)}) fusion(f32[48,180,58]{2,0,1:T(8,128)S(1)} %fusion.42), kind=kLoop, calls=%fused_computation.47 | loop fusion | bytes 4008960 | tf_op jit(solution)/shard_map/transpose | solution.py:46
  124.2 4.4 copy.114
  130.3 2.1 slice_multiply_fusion.1
  132.4 15.1 %gather_fusion = bf16[5120,48]{1,0:T(8,128)(2,1)S(1)} fusion(bf16[48,5120]{0,1:T(8,128)(2,1)S(1)} %slice_multiply_fusion.1, s32[5120]{0:T(1024)S(1)} %get-tuple-element.19), kind=kCustom, calls=%fused_computation | custom fusion | bytes 1003520 | tf_op jit(solution)/shard_map/gather | solution.py:95
  148.1 4.9 %copy.115 = f32[48,29,180]{0,2,1:T(8,128)S(1)} copy(f32[48,29,180]{1,0,2:T(8,128)} %get-tuple-element.8) | data formatting | bytes 2004480 | tf_op jit(solution)/shard_map/reshape | solution.py:49
  154.7 2.1 slice_multiply_fusion
  156.8 15.1 %gather_fusion.1 = bf16[5120,48]{1,0:T(8,128)(2,1)S(1)} fusion(bf16[48,5120]{0,1:T(8,128)(2,1)S(1)} %slice_multiply_fusion, s32[5120]{0:T(1024)S(1)} %get-tuple-element.19), kind=kCustom, calls=%fused_computation.1 | custom fusion | bytes 1003520 | tf_op jit(solution)/shard_map/gather | solution.py:96
  178.0 6.4 %all-to-all-start = ((bf16[8,6,16,640]{3,2,1,0:T(8,128)(2,1)}), bf16[8,6,16,640]{3,2,1,0:T(8,128)(2,1)S(1)}, u32[]{:S(2)}, u32[]{:S(2)}) async-start(bf16[8,6,16,640]{3,2,1,0:T(8,128)(2,1)} %fusion.80), calls=%async_computation | async-start | bytes 1966080 | tf_op jit(solution)/shard_map/all_to_all | solution.py:104
  184.4 24.2 %all-to-all-done = bf16[8,6,16,640]{3,2,1,0:T(8,128)(2,1)S(1)} async-done(((bf16[8,6,16,640]{3,2,1,0:T(8,128)(2,1)}), bf16[8,6,16,640]{3,2,1,0:T(8,128)(2,1)S(1)}, u32[]{:S(2)}, u32[]{:S(2)}) %all-to-all-start) | async-done | bytes 983072 | tf_op jit(solution)/shard_map/all_to_all | solution.py:104
  210.0 26.1 %fusion.51 = f32[6,640,128]{2,0,1:T(8,128)S(1)} fusion(bf16[6,128,640]{1,0,2:T(8,128)(2,1)S(1)} %copy.97, bf16[128,640,128]{2,1,0:T(8,128)(2,1)} %param.5), kind=kOutput, calls=%fused_computation.61 | convolution fusion | flops 125829120 | bytes 23920640 | tf_op jit(solution)/shard_map/xrk,rkn->xkn/dot_general | solution.py:101
  237.6 45.9 %all-reduce.2.cloned.1.call-done = f32[2,640,128]{2,1,0:T(8,128)} async-done(((f32[2,640,128]{2,1,0:T(8,128)}), f32[2,640,128]{2,1,0:T(8,128)}) %all-reduce.2.cloned.1.call-update) | async-done | bytes 655376 | tf_op jit(solution)/shard_map/psum | solution.py:122
  284.7 50.4 %fusion.61 = f32[2,128,640]{1,0,2:T(2,128)S(1)} fusion(bf16[128,640,128]{2,1,0:T(8,128)(2,1)} %param.5, bf16[2,640,128]{2,1,0:T(8,128)(2,1)S(1)} %multiply_convert_fusion), kind=kOutput, calls=%fused_computation.73 | convolution fusion | flops 41943040 | bytes 21954560 | tf_op jit(solution)/shard_map/rkn,ckn->crk/dot_general | solution.py:124
  336.5 5.3 %all-to-all-start.1 = ((f32[2,128,640]{2,0,1:T(2,128)}), f32[2,128,640]{2,0,1:T(2,128)S(1)}, u32[]{:S(2)}, u32[]{:S(2)}) async-start(f32[2,128,640]{2,0,1:T(2,128)} %copy.102), calls=%async_computation.1 | async-start | bytes 1310720 | tf_op jit(solution)/shard_map/all_to_all | solution.py:125
  341.8 26.6 %fusion.31 = (f32[180,29,240]{2,1,0:T(8,128)}, f32[180,29,240]{2,1,0:T(8,128)}, f32[180,29,240]{2,1,0:T(8,128)}) fusion(s32[29,240]{1,0:T(8,128)S(1)} %iota_multiply_fusion.2, s32[180,240]{1,0:T(8,128)S(1)} %iota_multiply_fusion), kind=kLoop, calls=%fused_computation.42 | loop fusion | flops 12528000 | bytes 15234240 | tf_op jit(solution)/shard_map/sin | solution.py:28
  368.5 2.2 copy.105
  370.8 14.0 %scatter_custom_fusion = f32[16,5220]{0,1:T(8,128)S(1)} fusion(s32[5120]{0:T(1024)S(1)} %get-tuple-element.20, f32[5120,16]{1,0:T(8,128)} %copy.105, f32[]{:T(128)} %constant.52.clone.1), kind=kCustom, calls=%fused_computation.69 | custom fusion | bytes 334592 | tf_op jit(solution)/shard_map/scatter | solution.py:129
  386.2 2.0 copy.107
  388.3 2.2 copy.109
  390.5 14.0 %scatter_custom_fusion.1 = f32[16,5220]{0,1:T(8,128)S(1)} fusion(s32[5120]{0:T(1024)S(1)} %get-tuple-element.20, f32[5120,16]{1,0:T(8,128)} %copy.109, f32[]{:T(128)} %constant.52.clone.1), kind=kCustom, calls=%fused_computation.67 | custom fusion | bytes 334592 | tf_op jit(solution)/shard_map/scatter | solution.py:132
  406.0 2.0 copy.111
  408.0 24.0 %fusion.39 = f32[16,180,480]{2,0,1:T(8,128)S(1)} fusion(f32[180,29,240]{2,1,0:T(8,128)} %get-tuple-element.18, f32[180,29,240]{2,1,0:T(8,128)} %get-tuple-element.17, f32[180,29,240]{2,1,0:T(8,128)} %get-tuple-element.16, f32[16,180,29]{2,0,1:T(8,128)} %bitcast.113, f32[16,180,29]{2,0,1:T(8,128)} %bitcast.112), kind=kOutput, calls=%fused_computation.56 | convolution fusion | flops 977351040 | bytes 21231360 | tf_op jit(solution)/shard_map/rkq,kqj->rkj/dot_general | solution.py:70
  433.1 4.9 %fusion.35 = f32[180,16,240]{2,0,1:T(8,128)S(1)} fusion(f32[16,180,240]{2,0,1:T(8,128)S(1)} %get-tuple-element.6), kind=kOutput, calls=%fused_computation.49 | convolution fusion | flops 1493283584 | bytes 5529600 | tf_op jit(solution)/shard_map/rkj,ka->raj/dot_general | solution.py:73
  438.0 5.1 %multiply_bitcast_fusion = f32[16,180,240]{2,1,0:T(8,128)S(1)} fusion(f32[180,16,240]{2,0,1:T(8,128)S(1)} %fusion.35, f32[16,180,240]{2,0,1:T(8,128)S(1)} %get-tuple-element.5), kind=kOutput, calls=%fused_computation.53 | convolution fusion | flops 1494665984 | bytes 8294400 | tf_op jit(solution)/shard_map/rkj,ka->raj/dot_general | solution.py:72
  443.2 2.5 mul.334
  (51 shorter events, 19.8 us)
Async XLA Ops:
  6.5 1.8 copy-start.1
  23.5 13.0 %copy-start = (f32[48,180,240]{2,1,0:T(8,128)S(1)}, f32[48,180,240]{2,1,0:T(8,128)}, u32[]{:S(2)}) copy-start(f32[48,180,240]{2,1,0:T(8,128)} %reshape.135) | copy-start | bytes 24883204
  128.6 3.8 copy-start.2
  178.0 30.6 %all-to-all-start = ((bf16[8,6,16,640]{3,2,1,0:T(8,128)(2,1)}), bf16[8,6,16,640]{3,2,1,0:T(8,128)(2,1)S(1)}, u32[]{:S(2)}, u32[]{:S(2)}) async-start(bf16[8,6,16,640]{3,2,1,0:T(8,128)(2,1)} %fusion.80), calls=%async_computation | async-start | bytes 1966080 | tf_op jit(solution)/shard_map/all_to_all | solution.py:104
  184.3 99.2 %all-reduce.2.cloned.1.call-start = ((), (), s32[]{:S(2)}) async-start(), calls=%async_computation.2 | async-start | bytes 1310720 | tf_op jit(solution)/shard_map/psum | solution.py:122
  236.0 1.4 copy-start.3
  336.5 32.0 %all-to-all-start.1 = ((f32[2,128,640]{2,0,1:T(2,128)}), f32[2,128,640]{2,0,1:T(2,128)S(1)}, u32[]{:S(2)}, u32[]{:S(2)}) async-start(f32[2,128,640]{2,0,1:T(2,128)} %copy.102), calls=%async_computation.1 | async-start | bytes 1310720 | tf_op jit(solution)/shard_map/all_to_all | solution.py:125
Sparse Core Ops, SparseCore 0:
  237.6 45.9 all-reduce.1
